TPU v7x, 256 devices: a whole 4x4x8 slice. The times are simulated.
256 devices in a mesh: group: 4 (over y), expert: 64 (over z, x, core).
Axes of the slice: x: 4, y: 4, z: 8, core: 2. Of those that a mesh axis runs over, the one named last changes fastest.
Arguments:
- tokens: bfloat16 [1024, 7168], P(('group', 'expert')), may hold values from -6 to 6
- expert_ids: int32 [1024, 8], P(('group', 'expert')), may hold values from 0 to 31, all different within a row; in each aligned block of 4 rows (0 to 3, 4 to 7, ...) at most 2 rows name the same one
- gate_weights: bfloat16 [1024, 8], P(('group', 'expert')), may hold values from 0.049804688 to 0.5
- w_gate: bfloat16 [256, 7168, 256], P(('group', 'expert')), may hold values from -0.0625 to 0.0625
- w_up: bfloat16 [256, 7168, 256], P(('group', 'expert')), may hold values from -0.0625 to 0.0625
- w_down: bfloat16 [256, 256, 7168], P(('group', 'expert')), may hold values from -0.125 to 0.125
Outputs:
- mixed: bfloat16 [1024, 7168], P(('group', 'expert'))
Inputs may be any that keep to these rules, and one draw needn't show every extreme that they name: `expert_ids`: each row names 8 different experts. Among the 4 rows of one device no expert is named by more than 2 rows, and in some device some expert is named by exactly 2 rows.
All inputs are finite; a program needn't handle non-finite values.
Results may differ from a plain program's by a relative error of at most 0.014.
Values may be sent and summed in bfloat16 or wider, within the bound.
A program may use at most 128 MiB of HBM per device.

v0:
```python
import jax
import jax.numpy as jnp
from jax import lax
from jax.sharding import PartitionSpec as P

EXP_GRP = 8
CAP = 2


def route_tables(expert_ids, gate_weights, experts, capacity):
    count = expert_ids.shape[0]
    labels = jnp.arange(experts, dtype=jnp.int32)
    match = expert_ids[:, :, None] == labels[None, None, :]
    named = jnp.any(match, axis=1).astype(jnp.float32)
    weight = jnp.sum(
        jnp.where(match, gate_weights.astype(jnp.float32)[:, :, None], jnp.float32(0.0)), axis=1
    )
    earlier = (jnp.arange(count)[:, None] > jnp.arange(count)[None, :]).astype(jnp.float32)
    rank = jnp.dot(earlier, named, precision=lax.Precision.HIGHEST)
    places = jnp.arange(capacity, dtype=jnp.float32)
    select = named[:, :, None] * (rank[:, :, None] == places[None, None, :]).astype(jnp.float32)
    return (select, select * weight[:, :, None])


def hidden_rows(flat, gate_block, up_block):
    gate_val = jnp.dot(flat, gate_block, preferred_element_type=jnp.float32)
    up_val = jnp.dot(flat, up_block, preferred_element_type=jnp.float32)
    return (jax.nn.silu(gate_val) * up_val).astype(jnp.bfloat16)


def expert_rows(flat, gate_block, up_block, down_block):
    hidden = hidden_rows(flat, gate_block, up_block)
    return jnp.dot(hidden, down_block, preferred_element_type=jnp.float32).astype(jnp.bfloat16)


def fold_blocks(returned, split):
    shape = returned.shape
    sectioned = returned.reshape(shape[0], shape[1] // split, split, shape[2], shape[3])
    return jnp.sum(sectioned, axis=2, dtype=jnp.float32).astype(jnp.bfloat16)


def weigh_slots(mixing, expert_out):
    return jnp.einsum(
        "rec,ecd->rd", mixing, expert_out.astype(jnp.float32), precision=lax.Precision.HIGHEST
    ).astype(jnp.bfloat16)


def on_device(tokens, expert_ids, gate_weights, w_gate, w_up, w_down):
    groups = lax.axis_size("group")
    members = lax.axis_size("expert")
    split = members // EXP_GRP
    experts = groups * EXP_GRP
    width = tokens.shape[1]
    select, mixing = route_tables(expert_ids, gate_weights, experts, CAP)
    outbound = jnp.einsum(
        "rec,rd->ecd", select, tokens.astype(jnp.float32), precision=lax.Precision.HIGHEST
    ).astype(jnp.bfloat16)
    boxes = outbound.reshape(groups, EXP_GRP, CAP, width)
    copies = jnp.repeat(boxes, split, axis=1)
    arrived = lax.all_to_all(
        lax.all_to_all(copies, "group", split_axis=0, concat_axis=0, tiled=True),
        "expert",
        split_axis=1,
        concat_axis=1,
        tiled=True,
    )
    flat = arrived.reshape(-1, width)
    partial_value = expert_rows(flat, w_gate[0], w_up[0], w_down[0])
    partial_value = partial_value.reshape(arrived.shape)
    returned = lax.all_to_all(
        lax.all_to_all(partial_value, "group", split_axis=0, concat_axis=0, tiled=True),
        "expert",
        split_axis=1,
        concat_axis=1,
        tiled=True,
    )
    expert_out = fold_blocks(returned, split)
    mixed = weigh_slots(mixing, expert_out.reshape(experts, CAP, width))
    return mixed


def solution(mesh):
    in_specs = (
        P(("group", "expert"), None),
        P(("group", "expert"), None),
        P(("group", "expert"), None),
        P(("group", "expert"), None, None),
        P(("group", "expert"), None, None),
        P(("group", "expert"), None, None),
    )
    out_specs = P(("group", "expert"), None)
    return jax.shard_map(
        on_device, mesh=mesh, in_specs=in_specs, out_specs=out_specs, check_vma=False
    )
```

profile of v0, /device:TPU:6, one launch (start us, length us, event | category | flops | bytes accessed | tf_op | source)
XLA Modules:
  0.0 609.0 jit_solution(15951842067546957721)
XLA Ops:
  0.0 0.0 copy-start
  0.0 0.8 fusion.18
  0.8 0.1 fusion.27
  0.9 0.0 copy-done
  0.9 1.0 fusion
  1.9 0.9 copy.23
  2.8 4.2 broadcast_in_dim.16
  7.0 86.8 %all_to_all.20 = bf16[4,64,2,7168]{3,2,1,0:T(2,128)(2,1)S(1)} all-to-all(bf16[4,64,2,7168]{3,2,1,0:T(2,128)(2,1)S(1)} %bitcast.31), channel_id=1, replica_groups=mesh['group'=4,'expert'=64] {'group'}, dimensions={0} | all-to-all | bytes 14680064 | tf_op jit(solution)/shard_map/all_to_all | solution.py:61
  93.8 7.1 %copy.24 = bf16[4,64,2,7168]{3,2,0,1:T(2,128)(2,1)S(1)} copy(bf16[4,64,2,7168]{3,2,1,0:T(2,128)(2,1)S(1)} %all_to_all.20) | data formatting | bytes 14680064 | tf_op jit(solution)/shard_map/all_to_all | solution.py:61
  100.9 175.4 %all_to_all.21 = bf16[4,64,2,7168]{3,2,0,1:T(2,128)(2,1)S(1)} all-to-all(bf16[4,64,2,7168]{3,2,0,1:T(2,128)(2,1)S(1)} %copy.24), channel_id=1, replica_groups=mesh['group'=4,'expert'=64] {'expert'}, dimensions={1} | all-to-all | bytes 14680064 | tf_op jit(solution)/shard_map/all_to_all | solution.py:60
  276.3 6.2 %copy.25 = bf16[4,64,2,7168]{3,2,1,0:T(2,128)(2,1)} copy(bf16[4,64,2,7168]{3,2,0,1:T(2,128)(2,1)S(1)} %all_to_all.21) | data formatting | bytes 14680064 | tf_op jit(solution)/shard_map/all_to_all | solution.py:60
  282.5 15.4 %reshape.27 = bf16[512,7168]{1,0:T(8,128)(2,1)} reshape(bf16[4,64,2,7168]{3,2,1,0:T(2,128)(2,1)} %copy.25) | data formatting | bytes 14680064 | tf_op jit(solution)/shard_map/reshape | solution.py:67
  297.9 6.2 %fusion.5 = f32[512,256]{1,0:T(8,128)S(1)} fusion(bf16[512,7168]{1,0:T(8,128)(2,1)} %reshape.27, bf16[1,7168,256]{2,1,0:T(8,128)(2,1)} %param.9), kind=kOutput, calls=%fused_computation.9 | convolution fusion | flops 1879048192 | bytes 11534336 | tf_op jit(solution)/shard_map/dot_general | solution.py:26
  304.1 16.0 %convolution_convert_fusion = bf16[512,7168]{1,0:T(8,128)(2,1)} fusion(bf16[1,256,7168]{2,1,0:T(8,128)(2,1)} %param.11, bf16[512,7168]{1,0:T(8,128)(2,1)} %reshape.27, bf16[1,7168,256]{2,1,0:T(8,128)(2,1)} %param.10, f32[512,256]{1,0:T(8,128)S(1)} %fusion.5), kind=kOutput, calls=%fused_computation | convolution fusion | flops 3762552832 | bytes 22544384 | tf_op jit(solution)/shard_map/dot_general | solution.py:33
  320.1 14.9 %reshape.28 = bf16[4,64,2,7168]{3,2,1,0:T(2,128)(2,1)} reshape(bf16[512,7168]{1,0:T(8,128)(2,1)} %convolution_convert_fusion) | data formatting | bytes 14680064 | tf_op jit(solution)/shard_map/reshape | solution.py:69
  335.0 85.3 %all_to_all.22 = bf16[4,64,2,7168]{3,2,1,0:T(2,128)(2,1)S(1)} all-to-all(bf16[4,64,2,7168]{3,2,1,0:T(2,128)(2,1)} %reshape.28), channel_id=1, replica_groups=mesh['group'=4,'expert'=64] {'group'}, dimensions={0} | all-to-all | bytes 14680064 | tf_op jit(solution)/shard_map/all_to_all | solution.py:71
  420.3 8.9 %copy.26 = bf16[4,64,2,7168]{3,2,0,1:T(2,128)(2,1)} copy(bf16[4,64,2,7168]{3,2,1,0:T(2,128)(2,1)S(1)} %all_to_all.22) | data formatting | bytes 14680064 | tf_op jit(solution)/shard_map/all_to_all | solution.py:71
  429.2 0.0 copy-start.3
  429.2 0.0 copy-start.2
  429.2 7.4 %all-to-all-start.3 = ((bf16[4,64,2,7168]{3,2,0,1:T(2,128)(2,1)}), bf16[4,64,2,7168]{3,2,0,1:T(2,128)(2,1)}, u32[]{:S(2)}, u32[]{:S(2)}) async-start(bf16[4,64,2,7168]{3,2,0,1:T(2,128)(2,1)} %copy.26), calls=%async_computation.3 | async-start | bytes 14680064 | tf_op jit(solution)/shard_map/all_to_all | solution.py:70
  436.6 0.0 copy-done.3
  436.6 0.0 copy-start.1
  436.6 0.0 copy-done.2
  436.6 0.1 select_reduce_fusion
  436.7 161.7 %all-to-all-done.3 = bf16[4,64,2,7168]{3,2,0,1:T(2,128)(2,1)} async-done(((bf16[4,64,2,7168]{3,2,0,1:T(2,128)(2,1)}), bf16[4,64,2,7168]{3,2,0,1:T(2,128)(2,1)}, u32[]{:S(2)}, u32[]{:S(2)}) %all-to-all-start.3) | async-done | bytes 7340064 | tf_op jit(solution)/shard_map/all_to_all | solution.py:70
  598.4 8.7 %bitcast_reduce_fusion = bf16[4,8,2,7168]{3,2,0,1:T(2,128)(2,1)S(1)} fusion(bf16[4,64,2,7168]{3,2,0,1:T(2,128)(2,1)} %all-to-all-done.3), kind=kLoop, calls=%fused_computation.5 | loop fusion | flops 3211264 | bytes 8257536 | tf_op jit(solution)/shard_map/reduce_sum | solution.py:39
  607.1 0.6 copy.29
  607.8 1.2 fusion.1
  609.0 0.0 copy-done.1
  (2 shorter events, 0.0 us)
Async XLA Ops:
  0.0 0.9 copy-start
  429.2 7.4 %copy-start.3 = (bf16[4,8]{1,0:T(4,128)(2,1)S(1)}, bf16[4,8]{1,0:T(4,128)(2,1)}, u32[]{:S(2)}) copy-start(bf16[4,8]{1,0:T(4,128)(2,1)} %param.8) | copy-start | bytes 196
  429.2 7.4 %copy-start.2 = (s32[4,8]{1,0:T(4,128)S(1)}, s32[4,8]{1,0:T(4,128)}, u32[]{:S(2)}) copy-start(s32[4,8]{1,0:T(4,128)} %param.7) | copy-start | bytes 388
  429.2 169.2 %all-to-all-start.3 = ((bf16[4,64,2,7168]{3,2,0,1:T(2,128)(2,1)}), bf16[4,64,2,7168]{3,2,0,1:T(2,128)(2,1)}, u32[]{:S(2)}, u32[]{:S(2)}) async-start(bf16[4,64,2,7168]{3,2,0,1:T(2,128)(2,1)} %copy.26), calls=%async_computation.3 | async-start | bytes 14680064 | tf_op jit(solution)/shard_map/all_to_all | solution.py:70
  436.6 172.4 %copy-start.1 = (bf16[4,7168]{1,0:T(4,128)(2,1)S(1)}, bf16[4,7168]{1,0:T(4,128)(2,1)}, u32[]{:S(2)}) copy-start(bf16[4,7168]{1,0:T(4,128)(2,1)} %param.6) | copy-start | bytes 172036
where the time goes:
time: 612 us; the launch traced here: 609 us
  blocking collectives  347 us (57%)
  waiting for transfers between devices  162 us (26%)
  local copies, waits for them, and re-layouts  58.3 us (10%)
  matrix products  24.4 us (4%)
  other arithmetic  9.57 us (2%)
  starting transfers between devices  7.36 us (1%)
    all_to_all x1, blocking collectives, on_device(): lax.all_to_all(lax.all_to_all(copies, 'group', split_axis=0, concat_axis=...  175 us
    all_to_all x1, waiting for transfers between devices, on_device(): lax.all_to_all(lax.all_to_all(partial_value, 'group', split_axis=0, conca...  162 us
    all_to_all x1, blocking collectives, on_device(): lax.all_to_all(copies, 'group', split_axis=0, concat_axis=0, tiled=True)  86.8 us
    all_to_all x1, blocking collectives, on_device(): lax.all_to_all(partial_value, 'group', split_axis=0, concat_axis=0, tiled...  85.3 us
    dot_general x1, matrix products, expert_rows(): jnp.dot(hidden, down_block, preferred_element_type=jnp.float32)  16 us
    reshape x1, local copies, waits for them, and re-layouts, on_device(): flat = arrived.reshape(-1, width)  15.4 us
    reshape x1, local copies, waits for them, and re-layouts, on_device(): partial_value = partial_value.reshape(arrived.shape)  14.9 us
  transfers between devices with their start and end apart: 1, of which 1 were waited for; matrix products, arithmetic and copies ran while one was open for 0% of the time, Pallas kernels for 0%

commit v1 on v0

v1 whole, which is shorter than its diff:
```python
import functools

import jax
import jax.numpy as jnp
from jax import lax
from jax.experimental import pallas as pl
from jax.experimental.pallas import tpu as pltpu
from jax.sharding import PartitionSpec as P

EXP_GRP = 8
CAP = 2
CORES = 2
WIDTH = 1024
MESH = pl.DeviceIdType.MESH
F32 = jnp.float32
BF16 = jnp.bfloat16


def routing_table(ids, gates, experts):
    rows, top = ids.shape
    lane = lax.broadcasted_iota(jnp.int32, (rows, 128), 1)
    named = jnp.zeros((rows, 128), F32)
    weight = jnp.zeros((rows, 128), F32)
    for k in range(top):
        chosen = ids[:, k : k + 1]
        named = jnp.where(lane == chosen, F32(1.0), named)
        weight = jnp.where(lane == chosen + experts, gates[:, k : k + 1], weight)
    earlier = jnp.zeros((1, 128), F32)
    out = []
    for row in range(rows):
        mine = named[row : row + 1]
        out.append(mine * (F32(1.0) + earlier) + weight[row : row + 1])
        earlier = earlier + mine
    return out


def kernel(
    groups, zs, xs, rows, chunks,
    tok_ref, ids_ref, gates_ref, gate_hbm, up_hbm, down_hbm, out_ref,
    w_gate, w_up, w_down, zbuf, meta, rowbuf, sel, mix, ysend, arrived,
    acc_gate, acc_up, hidden, psend, pair, part, keep_b, keep_own,
    send_far, send_f, send_b, got_far, got_f, got_b, vsend, vbuf, msend, fbuf,
    w_sem, meta_sem, z_sem, y_sem, b_sem, f_sem, fwd_sem, core_sem,
    pair_sem, far_sem, rf_sem, rb_sem, v_sem, fin_sem, send_sem,
):
    y = lax.axis_index("group")
    member = lax.axis_index("expert")
    z = member // (xs * CORES)
    x = (member // CORES) % xs
    c = member % CORES
    other = 1 - c
    step = 1 - 2 * c
    xf = (x + step + xs) % xs
    xb = (x - step + xs) % xs
    far = (x + 2) % xs
    experts = groups * EXP_GRP
    slots = zs * CAP

    def at(y_, z_, x_, c_):
        return (y_, (z_ * xs + x_) * CORES + c_)

    z_peers = [(z + d) % zs for d in range(1, zs)]
    y_peers = [(y + d) % groups for d in range(1, groups)]

    def send(src, dst, which, recv, where):
        pltpu.make_async_remote_copy(
            src_ref=src, dst_ref=dst, send_sem=send_sem.at[which], recv_sem=recv,
            device_id=where, device_id_type=MESH,
        ).start()

    def wait(ref, sem):
        pltpu.make_async_copy(ref, ref, sem).wait()

    weights = [
        pltpu.make_async_copy(gate_hbm.at[0], w_gate, w_sem.at[0]),
        pltpu.make_async_copy(up_hbm.at[0], w_up, w_sem.at[1]),
    ]
    for copy in weights:
        copy.start()
    for k in range(chunks):
        pltpu.make_async_copy(
            down_hbm.at[0, :, pl.ds(k * WIDTH, WIDTH)], w_down.at[k], w_sem.at[2]
        ).start()

    barrier = pltpu.get_barrier_semaphore()
    partners = (
        [at(y, p, x, c) for p in z_peers]
        + [at(p, z, x, c) for p in y_peers]
        + [at(y, z, xf, c), at(y, z, xb, c), at(y, z, x, other)]
    )
    for p in partners:
        pl.semaphore_signal(barrier, inc=1, device_id=p, device_id_type=MESH)

    table = routing_table(ids_ref[...], gates_ref[...].astype(F32), experts)
    for row in range(rows):
        meta[z, row : row + 1, :] = table[row]
    for k in range(chunks):
        zbuf[k, z] = tok_ref[:, k * WIDTH : (k + 1) * WIDTH]
    acc_gate[...] = jnp.zeros_like(acc_gate)
    acc_up[...] = jnp.zeros_like(acc_up)
    pl.semaphore_wait(barrier, len(partners))

    for p in z_peers:
        send(meta.at[z], meta.at[z], 0, meta_sem, at(y, p, x, c))

    def send_tokens(k):
        for p in z_peers:
            send(zbuf.at[k, z], zbuf.at[k, z], 1, z_sem.at[k], at(y, p, x, c))

    send_tokens(0)
    if chunks > 1:
        send_tokens(1)

    wait(meta.at[pl.ds(0, zs - 1)], meta_sem)
    for p in range(zs):
        rowbuf[rows * p : rows * (p + 1), 0:128] = meta[p]
    line = rowbuf[:, 0:128]
    total = zs * rows
    lane = lax.broadcasted_iota(jnp.int32, (total, 128), 1)
    row_id = lax.broadcasted_iota(jnp.int32, (total, groups * slots), 0)
    col_id = lax.broadcasted_iota(jnp.int32, (total, groups * slots), 1)
    same = (row_id // rows) == ((col_id % slots) // CAP)
    place = (col_id % CAP + 1).astype(F32)
    pick = jnp.zeros((total, groups * slots), F32)
    blend = jnp.zeros((total, groups * slots), F32)
    for q in range(groups):
        expert = q * EXP_GRP + z
        code = jnp.sum(jnp.where(lane == expert, line, F32(0.0)), axis=1, keepdims=True)
        weight = jnp.sum(jnp.where(lane == expert + experts, line, F32(0.0)), axis=1, keepdims=True)
        hit = same & (col_id // slots == q) & (code == place)
        pick = jnp.where(hit, F32(1.0), pick)
        blend = jnp.where(hit, weight, blend)
    mix[...] = blend.astype(BF16)
    n = groups * slots
    eye = (
        lax.broadcasted_iota(jnp.int32, (n, n), 0) == lax.broadcasted_iota(jnp.int32, (n, n), 1)
    ).astype(F32).astype(BF16)
    sel[...] = lax.dot_general(
        eye, pick.astype(BF16), (((1,), (1,)), ((), ())), preferred_element_type=F32
    ).astype(BF16)

    def dispatch(t, carry):
        @pl.when(t < chunks)
        def _():
            k = t
            wait(zbuf.at[k, pl.ds(0, zs - 1)], z_sem.at[k])
            for p in range(zs):
                rowbuf[rows * p : rows * (p + 1), :] = zbuf[k, p].astype(F32)
            picked = jnp.dot(sel[...], rowbuf[...].astype(BF16), preferred_element_type=F32)
            ysend[k] = picked.astype(BF16).reshape(groups, slots, WIDTH)
            for p in y_peers:
                send(ysend.at[k, p], arrived.at[k, c, x, y], 2, y_sem.at[k], at(p, z, x, c))
            arrived[k, c, x, y] = ysend[k, y]

        @pl.when(t + 2 < chunks)
        def _():
            send_tokens(t + 2)

        @pl.when((t >= 1) & (t < chunks + 1))
        def _():
            k = t - 1
            wait(arrived.at[k, c, x, pl.ds(0, groups - 1)], y_sem.at[k])
            own = arrived.at[k, c, x]
            send(own, own, 3, b_sem.at[k], at(y, z, xf, c))
            send(own, own, 3, f_sem.at[k], at(y, z, xb, c))
            send(own, own, 4, core_sem.at[k], at(y, z, x, other))

        @pl.when((t >= 2) & (t < chunks + 2))
        def _():
            k = t - 2
            back = arrived.at[k, c, xb]
            wait(back, b_sem.at[k])
            send(back, back, 3, fwd_sem.at[k], at(y, z, xf, c))
            send(back, back, 4, core_sem.at[k], at(y, z, x, other))
            front = arrived.at[k, c, xf]
            wait(front, f_sem.at[k])
            send(front, front, 4, core_sem.at[k], at(y, z, x, other))

        @pl.when((t >= 3) & (t < chunks + 3))
        def _():
            k = t - 3
            block = arrived.at[k, c, far]
            wait(block, fwd_sem.at[k])
            send(block, block, 4, core_sem.at[k], at(y, z, x, other))

        @pl.when(t >= 4)
        def _():
            k = t - 4
            wait(arrived.at[k, other], core_sem.at[k])

            @pl.when(k == 0)
            def _():
                for copy in weights:
                    copy.wait()

            depth = pl.ds(pl.multiple_of(k * WIDTH, WIDTH), WIDTH)
            for half in range(CORES):
                flat = arrived[k, half].reshape(-1, WIDTH)
                acc_gate[half] += jnp.dot(flat, w_gate[depth, :], preferred_element_type=F32)
                acc_up[half] += jnp.dot(flat, w_up[depth, :], preferred_element_type=F32)

        return carry

    lax.fori_loop(0, chunks + 4, dispatch, 0)

    gate_val = acc_gate[...]
    hidden[...] = (gate_val / (F32(1.0) + jnp.exp(-gate_val)) * acc_up[...]).astype(BF16)
    wait(w_down, w_sem.at[2])

    def combine(t, carry):
        @pl.when(t < chunks)
        def _():
            k = t
            value = jnp.dot(hidden[other], w_down[k], preferred_element_type=F32)
            psend[k] = value.astype(BF16).reshape(psend.shape[1:])
            send(psend.at[k], pair.at[k], 5, pair_sem.at[k], at(y, z, x, other))

        @pl.when((t >= 1) & (t < chunks + 1))
        def _():
            k = t - 1
            value = jnp.dot(hidden[c], w_down[k], preferred_element_type=F32)
            part[...] = value.reshape(part.shape)
            wait(pair.at[k], pair_sem.at[k])
            send_far[k] = (part[far] + pair[k, far].astype(F32)).astype(BF16)
            send(send_far.at[k], got_far.at[k], 6, far_sem.at[k], at(y, z, xb, c))
            send_f[k] = (part[xf] + pair[k, xf].astype(F32)).astype(BF16)
            send(send_f.at[k], got_b.at[k], 9, rb_sem.at[k], at(y, z, xf, c))
            keep_b[k] = part[xb] + pair[k, xb].astype(F32)
            keep_own[k] = part[x] + pair[k, x].astype(F32)

        @pl.when((t >= 2) & (t < chunks + 2))
        def _():
            k = t - 2
            wait(got_far.at[k], far_sem.at[k])
            send_b[k] = (keep_b[k] + got_far[k].astype(F32)).astype(BF16)
            send(send_b.at[k], got_f.at[k], 10, rf_sem.at[k], at(y, z, xb, c))

        @pl.when((t >= 3) & (t < chunks + 3))
        def _():
            k = t - 3
            wait(got_b.at[k], rb_sem.at[k])
            wait(got_f.at[k], rf_sem.at[k])
            value = keep_own[k] + got_b[k].astype(F32) + got_f[k].astype(F32)
            vsend[k] = value.astype(BF16)
            for p in y_peers:
                send(vsend.at[k, p], vbuf.at[k, y], 7, v_sem.at[k], at(p, z, x, c))
            vbuf[k, y] = vsend[k, y]

        @pl.when((t >= 4) & (t < chunks + 4))
        def _():
            k = t - 4
            wait(vbuf.at[k, pl.ds(0, groups - 1)], v_sem.at[k])
            value = jnp.dot(mix[...], vbuf[k].reshape(-1, WIDTH), preferred_element_type=F32)
            for p in range(zs):
                msend[k, p] = value[rows * p : rows * (p + 1)].astype(BF16)
            for p in z_peers:
                send(msend.at[k, p], fbuf.at[k, z], 8, fin_sem.at[k], at(y, p, x, c))
            fbuf[k, z] = msend[k, z]

        @pl.when(t >= 5)
        def _():
            k = t - 5
            wait(fbuf.at[k, pl.ds(0, zs - 1)], fin_sem.at[k])
            value = fbuf[k, 0].astype(F32)
            for p in range(1, zs):
                value = value + fbuf[k, p].astype(F32)
            out_ref[:, pl.ds(pl.multiple_of(k * WIDTH, WIDTH), WIDTH)] = value.astype(BF16)

        return carry

    lax.fori_loop(0, chunks + 5, combine, 0)

    wait(meta.at[pl.ds(0, zs - 1)], send_sem.at[0])
    wait(zbuf.at[:, pl.ds(0, zs - 1)], send_sem.at[1])
    wait(ysend.at[:, pl.ds(0, groups - 1)], send_sem.at[2])
    wait(arrived.at[:, 0, pl.ds(0, 3)], send_sem.at[3])
    wait(arrived.at[:, 0], send_sem.at[4])
    wait(psend, send_sem.at[5])
    wait(send_far, send_sem.at[6])
    wait(send_f, send_sem.at[9])
    wait(send_b, send_sem.at[10])
    wait(vsend.at[:, pl.ds(0, groups - 1)], send_sem.at[7])
    wait(msend.at[:, pl.ds(0, zs - 1)], send_sem.at[8])


def on_device(tokens, expert_ids, gate_weights, w_gate, w_up, w_down):
    groups = lax.axis_size("group")
    members = lax.axis_size("expert")
    zs = EXP_GRP
    xs = members // (EXP_GRP * CORES)
    rows, width = tokens.shape
    block = w_gate.shape[2]
    chunks = width // WIDTH
    slots = zs * CAP
    shard = (groups, slots, WIDTH)
    vmem = pltpu.VMEM
    dma = pltpu.SemaphoreType.DMA
    in_vmem = pl.BlockSpec(memory_space=pltpu.VMEM)
    in_hbm = pl.BlockSpec(memory_space=pltpu.HBM)
    side = (CORES, xs * groups * slots, block)
    return pl.pallas_call(
        functools.partial(kernel, groups, zs, xs, rows, chunks),
        out_shape=jax.ShapeDtypeStruct((rows, width), BF16),
        in_specs=[in_vmem] * 3 + [in_hbm] * 3,
        out_specs=in_vmem,
        scratch_shapes=[
            vmem((width, block), BF16),
            vmem((width, block), BF16),
            vmem((chunks, block, WIDTH), BF16),
            vmem((chunks, zs, rows, WIDTH), BF16),
            vmem((zs, rows, 128), F32),
            vmem((zs * rows, WIDTH), F32),
            vmem((groups * slots, zs * rows), BF16),
            vmem((zs * rows, groups * slots), BF16),
            vmem((chunks,) + shard, BF16),
            vmem((chunks, CORES, xs) + shard, BF16),
            vmem(side, F32),
            vmem(side, F32),
            vmem(side, BF16),
            vmem((chunks, xs) + shard, BF16),
            vmem((chunks, xs) + shard, BF16),
            vmem((xs,) + shard, F32),
            vmem((chunks,) + shard, F32),
            vmem((chunks,) + shard, F32),
        ]
        + [vmem((chunks,) + shard, BF16)] * 8
        + [vmem((chunks, zs, rows, WIDTH), BF16)] * 2
        + [dma((3,)), dma]
        + [dma((chunks,))] * 12
        + [dma((11,))],
        compiler_params=pltpu.CompilerParams(
            collective_id=0, has_side_effects=True, vmem_limit_bytes=60 * 1024 * 1024
        ),
    )(tokens, expert_ids, gate_weights, w_gate, w_up, w_down)


def solution(mesh):
    in_specs = (
        P(("group", "expert"), None),
        P(("group", "expert"), None),
        P(("group", "expert"), None),
        P(("group", "expert"), None, None),
        P(("group", "expert"), None, None),
        P(("group", "expert"), None, None),
    )
    out_specs = P(("group", "expert"), None)
    return jax.shard_map(
        on_device, mesh=mesh, in_specs=in_specs, out_specs=out_specs, check_vma=False
    )
```

time: 612 us -> 100 us (0.16)
  blocking collectives: 347 us -> 0 us
  waiting for transfers between devices: 162 us -> 0 us
  Pallas kernels: 0 us -> 98.4 us
  local copies, waits for them, and re-layouts: 58.3 us -> 1.46 us
  matrix products: 24.4 us -> 0 us
  other arithmetic: 9.57 us -> 0 us
  starting transfers between devices: 7.36 us -> 0 us
    all_to_all x3 -> x0, blocking collectives: 347 us -> none  [the longest x1 175 us: on_device(): lax.all_to_all(lax.all_to_all(copies, 'group', split_axis=0, concat_axis=...]
    all_to_all x1 -> x0, waiting for transfers between devices: 162 us -> none  [on_device(): lax.all_to_all(lax.all_to_all(partial_value, 'group', split_axis=0, conca...]
    pallas_call x0 -> x1, Pallas kernels: none -> 98.4 us  [on_device(): pl.pallas_call(functools.partial(kernel, groups, zs, xs, rows, chunks), o...]
    reshape x3 -> x0, local copies, waits for them, and re-layouts: 31.3 us -> none  [the longest x1 15.4 us: on_device(): flat = arrived.reshape(-1, width)]
    dot_general x5 -> x0, matrix products: 24.4 us -> none  [the longest x1 16 us: expert_rows(): jnp.dot(hidden, down_block, preferred_element_type=jnp.float32)]
    all_to_all x3 -> x0, local copies, waits for them, and re-layouts: 22.2 us -> none  [the longest x1 8.9 us: on_device(): lax.all_to_all(partial_value, 'group', split_axis=0, concat_axis=0, tiled...]
    reduce_sum x2 -> x0, other arithmetic: 8.78 us -> none  [the longest x1 8.69 us: fold_blocks(): return jnp.sum(sectioned, axis=2, dtype=jnp.float32).astype(jnp.bfloat16)]
    all_to_all x1 -> x0, starting transfers between devices: 7.36 us -> none  [on_device(): lax.all_to_all(lax.all_to_all(partial_value, 'group', split_axis=0, conca...]
  transfers between devices with their start and end apart: 1 -> 0, of which waited for: 1 -> 0; matrix products, arithmetic and copies ran while one was open for 0% -> 0% of each run, Pallas kernels for 0% -> 0%
where the time goes in v1:
time: 100 us; the launch traced here: 99.8 us
  Pallas kernels  98.4 us (98%)
  local copies, waits for them, and re-layouts  1.46 us (1%)
    pallas_call x1, Pallas kernels, on_device(): pl.pallas_call(functools.partial(kernel, groups, zs, xs, rows, chunks), o...  98.4 us

profile of v1, /device:TPU:6, one launch (start us, length us, event | category | flops | bytes accessed | tf_op | source)
XLA Modules:
  0.0 99.8 jit_solution(2640159580964374377)
XLA Ops:
  0.0 98.4 %shard_map.64 = bf16[4,7168]{1,0:T(4,128)(2,1)} custom-call(bf16[4,7168]{1,0:T(4,128)(2,1)} %tok_ref.1, s32[4,8]{1,0:T(4,128)} %ids_ref.1, bf16[4,8]{1,0:T(4,128)(2,1)} %gates_ref.1, bf16[1,7168,256]{2,1,0:T(8,128)(2,1)} %gate_hbm.1, bf16[1,7168,256]{2,1,0:T(8,128)(2,1)} %up_hbm.1, bf16[1,256,7168]{2,1,0:T(8,128)(2,1)} %down_hbm.1), custom_call_target="tpu_custom_call" | custom-call | tf_op jit(solution)/shard_map/pallas_call | solution.py:301
  98.4 1.5 %copy.8 = bf16[4,7168]{1,0:T(4,128)(2,1)} copy(bf16[4,7168]{1,0:T(4,128)(2,1)} %shard_map.64) | data formatting | bytes 114688

commit v2 on v1

v2 whole, which is shorter than its diff:
```python
import functools

import jax
import jax.numpy as jnp
from jax import lax
from jax.experimental import pallas as pl
from jax.experimental.pallas import tpu as pltpu
from jax.sharding import PartitionSpec as P

EXP_GRP = 8
CAP = 2
CORES = 2
WIDTH = 512
WIDE = 5
AHEAD = 9
EARLY = 9
LAGS = (0, 2, 5, 8, 9)
WIDE_LAGS = (0, 6, 9, 10)
BACK_LAGS = (0, 2, 5, 8, 10, 12)
WIDE_BACK_LAGS = (0, 2, 5, 8, 11)
MESH = pl.DeviceIdType.MESH
F32 = jnp.float32
BF16 = jnp.bfloat16


def routing_table(ids, gates, experts):
    rows, top = ids.shape
    lane = lax.broadcasted_iota(jnp.int32, (rows, 128), 1)
    named = jnp.zeros((rows, 128), F32)
    weight = jnp.zeros((rows, 128), F32)
    for k in range(top):
        chosen = ids[:, k : k + 1]
        named = jnp.where(lane == chosen, F32(1.0), named)
        weight = jnp.where(lane == chosen + experts, gates[:, k : k + 1], weight)
    earlier = jnp.zeros((1, 128), F32)
    out = []
    for row in range(rows):
        mine = named[row : row + 1]
        out.append(mine * (F32(1.0) + earlier) + weight[row : row + 1])
        earlier = earlier + mine
    return out


def kernel(
    groups, zs, xs, rows, chunks,
    tok_ref, ids_ref, gates_ref, gate_hbm, up_hbm, down_hbm, out_ref,
    w_gate, w_up, w_down, zbuf, zwide, meta, rowbuf, sel, mix, ysend, ywide, arrived,
    acc_gate, acc_up, hidden, psend, pair, part, keep_b, keep_own,
    send_far, send_f, send_b, got_far, got_f, got_b, vsend, vbuf, msend, fbuf,
    vwide, vgot, mwide, fgot, hsend, hgot,
    w_sem, meta_sem, metax_sem, z_sem, y_sem, b_sem, f_sem, fwd_sem,
    far_sem, rf_sem, rb_sem, v_sem, fin_sem,
    xw_sem, zw_sem, yw_sem, vw_sem, fw_sem, hw_sem,
    core_sem, pair_sem, send_sem,
):
    y = lax.axis_index("group")
    member = lax.axis_index("expert")
    z = member // (xs * CORES)
    x = (member // CORES) % xs
    c = member % CORES
    other = 1 - c
    step = 1 - 2 * c
    xf = (x + step + xs) % xs
    xb = (x - step + xs) % xs
    far = (x + 2) % xs
    experts = groups * EXP_GRP
    slots = zs * CAP
    wide = min(WIDE, chunks - 1)
    ring = chunks - wide

    def at(y_, z_, x_, c_):
        return (y_, (z_ * xs + x_) * CORES + c_)

    z_peers = [(z + d) % zs for d in range(1, zs)]
    y_peers = [(y + d) % groups for d in range(1, groups)]
    x_peers = [(x + d) % xs for d in range(1, xs)]

    def send(src, dst, which, recv, where):
        pltpu.make_async_remote_copy(
            src_ref=src, dst_ref=dst, send_sem=send_sem.at[which], recv_sem=recv,
            device_id=where, device_id_type=MESH,
        ).start()

    def wait(ref, sem):
        pltpu.make_async_copy(ref, ref, sem).wait()

    def columns(k):
        return pl.ds(pl.multiple_of(k * WIDTH, WIDTH), WIDTH)

    weights = [
        pltpu.make_async_copy(gate_hbm.at[0], w_gate, w_sem.at[0]),
        pltpu.make_async_copy(up_hbm.at[0], w_up, w_sem.at[1]),
    ]
    for copy in weights:
        copy.start()
    for k in range(chunks):
        pltpu.make_async_copy(
            down_hbm.at[0, :, pl.ds(k * WIDTH, WIDTH)], w_down.at[k], w_sem.at[2]
        ).start()

    barrier = pltpu.get_barrier_semaphore()
    partners = (
        [at(y, p, x, c) for p in z_peers]
        + [at(p, z, x, c) for p in y_peers]
        + [at(y, z, p, c) for p in x_peers]
        + [at(y, z, x, other)]
    )
    for p in partners:
        pl.semaphore_signal(barrier, inc=1, device_id=p, device_id_type=MESH)

    table = routing_table(ids_ref[...], gates_ref[...].astype(F32), experts)
    for row in range(rows):
        meta[x, z, row : row + 1, :] = table[row]
    for k in range(ring):
        zbuf[k, z] = tok_ref[:, k * WIDTH : (k + 1) * WIDTH]
    for k in range(ring, chunks):
        zwide[k - ring, z, x] = tok_ref[:, k * WIDTH : (k + 1) * WIDTH]
    acc_gate[...] = jnp.zeros_like(acc_gate)
    acc_up[...] = jnp.zeros_like(acc_up)
    pl.semaphore_wait(barrier, len(partners))

    for p in z_peers:
        send(meta.at[x, z], meta.at[x, z], 0, meta_sem, at(y, p, x, c))

    def send_z(k):
        for p in z_peers:
            send(zbuf.at[k, z], zbuf.at[k, z], 1, z_sem.at[k], at(y, p, x, c))

    for k in range(EARLY):
        send_z(k)

    def first_wide(k, carry):
        for p in x_peers:
            send(zwide.at[k, z, x], zwide.at[k, z, x], 11, xw_sem.at[k], at(y, z, p, c))
        return carry

    lax.fori_loop(0, wide, first_wide, 0)

    total = zs * rows
    n = groups * slots
    lane = lax.broadcasted_iota(jnp.int32, (total, 128), 1)
    row_id = lax.broadcasted_iota(jnp.int32, (total, n), 0)
    col_id = lax.broadcasted_iota(jnp.int32, (total, n), 1)
    same = (row_id // rows) == ((col_id % slots) // CAP)
    place = (col_id % CAP + 1).astype(F32)
    eye = (
        lax.broadcasted_iota(jnp.int32, (n, n), 0) == lax.broadcasted_iota(jnp.int32, (n, n), 1)
    ).astype(F32).astype(BF16)

    def choose(p):
        for q in range(zs):
            rowbuf[rows * q : rows * (q + 1), 0:128] = meta[p, q]
        line = rowbuf[:, 0:128]
        pick = jnp.zeros((total, n), F32)
        blend = jnp.zeros((total, n), F32)
        for q in range(groups):
            expert = q * EXP_GRP + z
            code = jnp.sum(jnp.where(lane == expert, line, F32(0.0)), axis=1, keepdims=True)
            weight = jnp.sum(
                jnp.where(lane == expert + experts, line, F32(0.0)), axis=1, keepdims=True
            )
            hit = same & (col_id // slots == q) & (code == place)
            pick = jnp.where(hit, F32(1.0), pick)
            blend = jnp.where(hit, weight, blend)
        mix[p] = blend.astype(BF16)
        sel[p] = lax.dot_general(
            eye, pick.astype(BF16), (((1,), (1,)), ((), ())), preferred_element_type=F32
        ).astype(BF16)

    wait(meta.at[x, pl.ds(0, zs - 1)], meta_sem)
    for p in x_peers:
        send(meta.at[x], meta.at[x], 12, metax_sem, at(y, z, p, c))
    for k in range(EARLY, AHEAD):
        send_z(k)
    choose(x)

    def multiply(k):
        wait(arrived.at[k, other], core_sem.at[k])
        for half in range(CORES):
            flat = arrived[k, half].reshape(-1, WIDTH)
            acc_gate[half] += jnp.dot(flat, w_gate[columns(k), :], preferred_element_type=F32)
            acc_up[half] += jnp.dot(flat, w_up[columns(k), :], preferred_element_type=F32)

    def run(t, lag, count, body):
        @pl.when((t >= lag) & (t < lag + count))
        def _():
            body(t - lag)

    def pick_rows(k):
        wait(zbuf.at[k, pl.ds(0, zs - 1)], z_sem.at[k])
        for p in range(zs):
            rowbuf[rows * p : rows * (p + 1), :] = zbuf[k, p].astype(F32)
        picked = jnp.dot(sel[x], rowbuf[...].astype(BF16), preferred_element_type=F32)
        ysend[k] = picked.astype(BF16).reshape(groups, slots, WIDTH)
        for p in y_peers:
            send(ysend.at[k, p], arrived.at[k, c, x, y], 2, y_sem.at[k], at(p, z, x, c))
        arrived[k, c, x, y] = ysend[k, y]

    def ring_start(k):
        wait(arrived.at[k, c, x, pl.ds(0, groups - 1)], y_sem.at[k])
        own = arrived.at[k, c, x]
        send(own, own, 3, b_sem.at[k], at(y, z, xf, c))
        send(own, own, 3, f_sem.at[k], at(y, z, xb, c))
        send(own, own, 4, core_sem.at[k], at(y, z, x, other))

    def ring_forward(k):
        back = arrived.at[k, c, xb]
        wait(back, b_sem.at[k])
        send(back, back, 3, fwd_sem.at[k], at(y, z, xf, c))
        send(back, back, 4, core_sem.at[k], at(y, z, x, other))
        front = arrived.at[k, c, xf]
        wait(front, f_sem.at[k])
        send(front, front, 4, core_sem.at[k], at(y, z, x, other))

    def ring_end(k):
        block = arrived.at[k, c, far]
        wait(block, fwd_sem.at[k])
        send(block, block, 4, core_sem.at[k], at(y, z, x, other))

    def wide_z(j):
        wait(zwide.at[j, z, pl.ds(0, xs - 1)], xw_sem.at[j])
        for p in z_peers:
            send(zwide.at[j, z], zwide.at[j, z], 13, zw_sem.at[j], at(y, p, x, c))

    def wide_pick(j):
        @pl.when(j == 0)
        def _():
            wait(meta.at[pl.ds(0, xs - 1)], metax_sem)
            for p in x_peers:
                choose(p)

        wait(zwide.at[j, pl.ds(0, zs - 1)], zw_sem.at[j])
        k = ring + j
        for p in range(xs):
            for q in range(zs):
                rowbuf[rows * q : rows * (q + 1), :] = zwide[j, q, p].astype(F32)
            picked = jnp.dot(sel[p], rowbuf[...].astype(BF16), preferred_element_type=F32)
            picked = picked.astype(BF16).reshape(groups, slots, WIDTH)
            for q in range(groups):
                ywide[j, q, p] = picked[q]
        for p in y_peers:
            send(ywide.at[j, p], arrived.at[k, c, :, y], 14, yw_sem.at[j], at(p, z, x, c))
        for p in range(xs):
            arrived[k, c, p, y] = ywide[j, y, p]

    def wide_share(j):
        k = ring + j
        wait(arrived.at[k, c, pl.ds(0, groups - 1)], yw_sem.at[j])
        block = arrived.at[k, c]
        send(block, block, 4, core_sem.at[k], at(y, z, x, other))

    def loaded(j):
        for copy in weights:
            copy.wait()

    def dispatch(t, carry):
        run(t, LAGS[0], ring, pick_rows)
        run(t, LAGS[0], ring - AHEAD, lambda k: send_z(k + AHEAD))
        run(t, LAGS[1], ring, ring_start)
        run(t, WIDE_LAGS[0], wide, wide_z)
        run(t, LAGS[2], ring, ring_forward)
        run(t, WIDE_LAGS[1], wide, wide_pick)
        run(t, LAGS[3], ring, ring_end)
        run(t, WIDE_LAGS[2], wide, wide_share)
        run(t, min(LAGS[-1], WIDE_LAGS[-1]), 1, loaded)
        run(t, LAGS[4], ring, multiply)
        run(t, WIDE_LAGS[3], wide, lambda j: multiply(ring + j))
        return carry

    lax.fori_loop(0, max(ring + LAGS[-1], wide + WIDE_LAGS[-1]), dispatch, 0)

    gate_val = acc_gate[...]
    hidden[...] = (gate_val / (F32(1.0) + jnp.exp(-gate_val)) * acc_up[...]).astype(BF16)
    wait(w_down, w_sem.at[2])

    def partial_sum(k):
        value = jnp.dot(hidden[other], w_down[k], preferred_element_type=F32)
        psend[k] = value.astype(BF16).reshape(psend.shape[1:])
        send(psend.at[k], pair.at[k], 5, pair_sem.at[k], at(y, z, x, other))

    def reduce_start(k):
        value = jnp.dot(hidden[c], w_down[k], preferred_element_type=F32)
        part[...] = value.reshape(part.shape)
        wait(pair.at[k], pair_sem.at[k])
        send_far[k] = (part[far] + pair[k, far].astype(F32)).astype(BF16)
        send(send_far.at[k], got_far.at[k], 6, far_sem.at[k], at(y, z, xb, c))
        send_f[k] = (part[xf] + pair[k, xf].astype(F32)).astype(BF16)
        send(send_f.at[k], got_b.at[k], 9, rb_sem.at[k], at(y, z, xf, c))
        keep_b[k] = part[xb] + pair[k, xb].astype(F32)
        keep_own[k] = part[x] + pair[k, x].astype(F32)

    def reduce_forward(k):
        wait(got_far.at[k], far_sem.at[k])
        send_b[k] = (keep_b[k] + got_far[k].astype(F32)).astype(BF16)
        send(send_b.at[k], got_f.at[k], 10, rf_sem.at[k], at(y, z, xb, c))

    def reduce_end(k):
        wait(got_b.at[k], rb_sem.at[k])
        wait(got_f.at[k], rf_sem.at[k])
        value = keep_own[k] + got_b[k].astype(F32) + got_f[k].astype(F32)
        vsend[k] = value.astype(BF16)
        for p in y_peers:
            send(vsend.at[k, p], vbuf.at[k, y], 7, v_sem.at[k], at(p, z, x, c))
        vbuf[k, y] = vsend[k, y]

    def blend_rows(k):
        wait(vbuf.at[k, pl.ds(0, groups - 1)], v_sem.at[k])
        value = jnp.dot(mix[x], vbuf[k].reshape(-1, WIDTH), preferred_element_type=F32)
        for p in range(zs):
            msend[k, p] = value[rows * p : rows * (p + 1)].astype(BF16)
        for p in z_peers:
            send(msend.at[k, p], fbuf.at[k, z], 8, fin_sem.at[k], at(y, p, x, c))
        fbuf[k, z] = msend[k, z]

    def finish(k):
        wait(fbuf.at[k, pl.ds(0, zs - 1)], fin_sem.at[k])
        value = fbuf[k, 0].astype(F32)
        for p in range(1, zs):
            value = value + fbuf[k, p].astype(F32)
        out_ref[:, columns(k)] = value.astype(BF16)

    def wide_back(j):
        k = ring + j
        value = jnp.dot(hidden[c], w_down[k], preferred_element_type=F32)
        part[...] = value.reshape(part.shape)
        wait(pair.at[k], pair_sem.at[k])
        for p in range(xs):
            summed = (part[p] + pair[k, p].astype(F32)).astype(BF16)
            for q in range(groups):
                vwide[j, q, p] = summed[q]
        for p in y_peers:
            send(vwide.at[j, p], vgot.at[j, y], 15, vw_sem.at[j], at(p, z, x, c))
        vgot[j, y] = vwide[j, y]

    def wide_blend(j):
        wait(vgot.at[j, pl.ds(0, groups - 1)], vw_sem.at[j])
        for p in range(xs):
            value = jnp.dot(mix[p], vgot[j, :, p].reshape(-1, WIDTH), preferred_element_type=F32)
            for q in range(zs):
                mwide[j, q, p] = value[rows * q : rows * (q + 1)].astype(BF16)
        for p in z_peers:
            send(mwide.at[j, p], fgot.at[j, z], 16, fw_sem.at[j], at(y, p, x, c))
        fgot[j, z] = mwide[j, z]

    def wide_sum(j):
        wait(fgot.at[j, pl.ds(0, zs - 1)], fw_sem.at[j])
        value = fgot[j, 0].astype(F32)
        for p in range(1, zs):
            value = value + fgot[j, p].astype(F32)
        hsend[j] = value.astype(BF16)
        for p in x_peers:
            send(hsend.at[j, p], hgot.at[j, x], 17, hw_sem.at[j], at(y, z, p, c))
        hgot[j, x] = hsend[j, x]

    def wide_finish(j):
        wait(hgot.at[j, pl.ds(0, xs - 1)], hw_sem.at[j])
        value = hgot[j, 0].astype(F32)
        for p in range(1, xs):
            value = value + hgot[j, p].astype(F32)
        out_ref[:, columns(ring + j)] = value.astype(BF16)

    def combine(t, carry):
        run(t, BACK_LAGS[0], ring, partial_sum)
        run(t, WIDE_BACK_LAGS[0], wide, lambda j: partial_sum(ring + j))
        run(t, BACK_LAGS[1], ring, reduce_start)
        run(t, WIDE_BACK_LAGS[1], wide, wide_back)
        run(t, BACK_LAGS[2], ring, reduce_forward)
        run(t, WIDE_BACK_LAGS[2], wide, wide_blend)
        run(t, BACK_LAGS[3], ring, reduce_end)
        run(t, WIDE_BACK_LAGS[3], wide, wide_sum)
        run(t, BACK_LAGS[4], ring, blend_rows)
        run(t, WIDE_BACK_LAGS[4], wide, wide_finish)
        run(t, BACK_LAGS[5], ring, finish)
        return carry

    lax.fori_loop(0, max(ring + BACK_LAGS[-1], wide + WIDE_BACK_LAGS[-1]), combine, 0)

    wait(meta.at[x, pl.ds(0, zs - 1)], send_sem.at[0])
    wait(zbuf.at[:, pl.ds(0, zs - 1)], send_sem.at[1])
    wait(ysend.at[:, pl.ds(0, groups - 1)], send_sem.at[2])
    wait(arrived.at[pl.ds(0, ring), 0, pl.ds(0, 3)], send_sem.at[3])
    wait(arrived.at[:, 0], send_sem.at[4])
    wait(psend, send_sem.at[5])
    wait(send_far, send_sem.at[6])
    wait(vsend.at[:, pl.ds(0, groups - 1)], send_sem.at[7])
    wait(msend.at[:, pl.ds(0, zs - 1)], send_sem.at[8])
    wait(send_f, send_sem.at[9])
    wait(send_b, send_sem.at[10])
    wait(zwide.at[:, 0, pl.ds(0, xs - 1)], send_sem.at[11])
    wait(meta.at[pl.ds(0, xs - 1)], send_sem.at[12])
    wait(zwide.at[:, pl.ds(0, zs - 1)], send_sem.at[13])
    wait(ywide.at[:, pl.ds(0, groups - 1)], send_sem.at[14])
    wait(vwide.at[:, pl.ds(0, groups - 1)], send_sem.at[15])
    wait(mwide.at[:, pl.ds(0, zs - 1)], send_sem.at[16])
    wait(hsend.at[:, pl.ds(0, xs - 1)], send_sem.at[17])


def on_device(tokens, expert_ids, gate_weights, w_gate, w_up, w_down):
    groups = lax.axis_size("group")
    members = lax.axis_size("expert")
    zs = EXP_GRP
    xs = members // (EXP_GRP * CORES)
    rows, width = tokens.shape
    block = w_gate.shape[2]
    chunks = width // WIDTH
    wide = min(WIDE, chunks - 1)
    ring = chunks - wide
    slots = zs * CAP
    shard = (groups, slots, WIDTH)
    vmem = pltpu.VMEM
    dma = pltpu.SemaphoreType.DMA
    in_vmem = pl.BlockSpec(memory_space=pltpu.VMEM)
    in_hbm = pl.BlockSpec(memory_space=pltpu.HBM)
    side = (CORES, xs * groups * slots, block)
    return pl.pallas_call(
        functools.partial(kernel, groups, zs, xs, rows, chunks),
        out_shape=jax.ShapeDtypeStruct((rows, width), BF16),
        in_specs=[in_vmem] * 3 + [in_hbm] * 3,
        out_specs=in_vmem,
        scratch_shapes=[
            vmem((width, block), BF16),
            vmem((width, block), BF16),
            vmem((chunks, block, WIDTH), BF16),
            vmem((ring, zs, rows, WIDTH), BF16),
            vmem((wide, zs, xs, rows, WIDTH), BF16),
            vmem((xs, zs, rows, 128), F32),
            vmem((zs * rows, WIDTH), F32),
            vmem((xs, groups * slots, zs * rows), BF16),
            vmem((xs, zs * rows, groups * slots), BF16),
            vmem((ring,) + shard, BF16),
            vmem((wide, groups, xs, slots, WIDTH), BF16),
            vmem((chunks, CORES, xs) + shard, BF16),
            vmem(side, F32),
            vmem(side, F32),
            vmem(side, BF16),
            vmem((chunks, xs) + shard, BF16),
            vmem((chunks, xs) + shard, BF16),
            vmem((xs,) + shard, F32),
            vmem((ring,) + shard, F32),
            vmem((ring,) + shard, F32),
        ]
        + [vmem((ring,) + shard, BF16)] * 8
        + [vmem((ring, zs, rows, WIDTH), BF16)] * 2
        + [vmem((wide, groups, xs, slots, WIDTH), BF16)] * 2
        + [vmem((wide, zs, xs, rows, WIDTH), BF16)] * 2
        + [vmem((wide, xs, rows, WIDTH), BF16)] * 2
        + [dma((3,)), dma, dma]
        + [dma((ring,))] * 10
        + [dma((wide,))] * 6
        + [dma((chunks,))] * 2
        + [dma((18,))],
        compiler_params=pltpu.CompilerParams(
            collective_id=0, has_side_effects=True, vmem_limit_bytes=60 * 1024 * 1024
        ),
    )(tokens, expert_ids, gate_weights, w_gate, w_up, w_down)


def solution(mesh):
    in_specs = (
        P(("group", "expert"), None),
        P(("group", "expert"), None),
        P(("group", "expert"), None),
        P(("group", "expert"), None, None),
        P(("group", "expert"), None, None),
        P(("group", "expert"), None, None),
    )
    out_specs = P(("group", "expert"), None)
    return jax.shard_map(
        on_device, mesh=mesh, in_specs=in_specs, out_specs=out_specs, check_vma=False
    )
```

time: 100 us -> 90 us (0.900)
  Pallas kernels: 98.4 us -> 87.7 us
    pallas_call x1, Pallas kernels: 98.4 us -> 87.7 us  [on_device(): pl.pallas_call(functools.partial(kernel, groups, zs, xs, rows, chunks), o...]
where the time goes in v2:
time: 90 us; the launch traced here: 89.2 us
  Pallas kernels  87.7 us (97%)
  local copies, waits for them, and re-layouts  1.46 us (2%)
    pallas_call x1, Pallas kernels, on_device(): pl.pallas_call(functools.partial(kernel, groups, zs, xs, rows, chunks), o...  87.7 us

profile of v2, /device:TPU:6, one launch (start us, length us, event | category | flops | bytes accessed | tf_op | source)
XLA Modules:
  0.0 89.2 jit_solution(5690481263026442314)
XLA Ops:
  0.0 87.7 %shard_map.64 = bf16[4,7168]{1,0:T(4,128)(2,1)} custom-call(bf16[4,7168]{1,0:T(4,128)(2,1)} %tok_ref.1, s32[4,8]{1,0:T(4,128)} %ids_ref.1, bf16[4,8]{1,0:T(4,128)(2,1)} %gates_ref.1, bf16[1,7168,256]{2,1,0:T(8,128)(2,1)} %gate_hbm.1, bf16[1,7168,256]{2,1,0:T(8,128)(2,1)} %up_hbm.1, bf16[1,256,7168]{2,1,0:T(8,128)(2,1)} %down_hbm.1), custom_call_target="tpu_custom_call" | custom-call | tf_op jit(solution)/shard_map/pallas_call | solution.py:415
  87.7 1.5 %copy.8 = bf16[4,7168]{1,0:T(4,128)(2,1)} copy(bf16[4,7168]{1,0:T(4,128)(2,1)} %shard_map.64) | data formatting | bytes 114688

commit v3 on v2

--- a/solution.py
+++ b/solution.py
@@ -12,12 +12,14 @@
 CORES = 2
 WIDTH = 512
 WIDE = 5
+DIRECT = 1
+STRIDE = 2
 AHEAD = 9
 EARLY = 9
 LAGS = (0, 2, 5, 8, 9)
-WIDE_LAGS = (0, 6, 9, 10)
+WIDE_LAGS = (0, 5, 8, 9)
 BACK_LAGS = (0, 2, 5, 8, 10, 12)
-WIDE_BACK_LAGS = (0, 2, 5, 8, 11)
+WIDE_BACK_LAGS = (0, 1, 5, 9, 12)
 MESH = pl.DeviceIdType.MESH
 F32 = jnp.float32
 BF16 = jnp.bfloat16
@@ -67,6 +69,7 @@
     slots = zs * CAP
     wide = min(WIDE, chunks - 1)
     ring = chunks - wide
+    relayed = ring - DIRECT
 
     def at(y_, z_, x_, c_):
         return (y_, (z_ * xs + x_) * CORES + c_)
@@ -186,6 +189,11 @@
         def _():
             body(t - lag)
 
+    def run_wide(t, lag, body):
+        @pl.when((t >= lag) & (t < lag + wide * STRIDE) & ((t - lag) % STRIDE == 0))
+        def _():
+            body((t - lag) // STRIDE)
+
     def pick_rows(k):
         wait(zbuf.at[k, pl.ds(0, zs - 1)], z_sem.at[k])
         for p in range(zs):
@@ -203,10 +211,18 @@
         send(own, own, 3, f_sem.at[k], at(y, z, xb, c))
         send(own, own, 4, core_sem.at[k], at(y, z, x, other))
 
+        @pl.when(k >= relayed)
+        def _():
+            send(own, own, 3, fwd_sem.at[k], at(y, z, far, c))
+
     def ring_forward(k):
         back = arrived.at[k, c, xb]
         wait(back, b_sem.at[k])
-        send(back, back, 3, fwd_sem.at[k], at(y, z, xf, c))
+
+        @pl.when(k < relayed)
+        def _():
+            send(back, back, 3, fwd_sem.at[k], at(y, z, xf, c))
+
         send(back, back, 4, core_sem.at[k], at(y, z, x, other))
         front = arrived.at[k, c, xf]
         wait(front, f_sem.at[k])
@@ -257,17 +273,17 @@
         run(t, LAGS[0], ring, pick_rows)
         run(t, LAGS[0], ring - AHEAD, lambda k: send_z(k + AHEAD))
         run(t, LAGS[1], ring, ring_start)
-        run(t, WIDE_LAGS[0], wide, wide_z)
+        run_wide(t, WIDE_LAGS[0], wide_z)
         run(t, LAGS[2], ring, ring_forward)
-        run(t, WIDE_LAGS[1], wide, wide_pick)
+        run_wide(t, WIDE_LAGS[1], wide_pick)
         run(t, LAGS[3], ring, ring_end)
-        run(t, WIDE_LAGS[2], wide, wide_share)
+        run_wide(t, WIDE_LAGS[2], wide_share)
         run(t, min(LAGS[-1], WIDE_LAGS[-1]), 1, loaded)
         run(t, LAGS[4], ring, multiply)
-        run(t, WIDE_LAGS[3], wide, lambda j: multiply(ring + j))
+        run_wide(t, WIDE_LAGS[3], lambda j: multiply(ring + j))
         return carry
 
-    lax.fori_loop(0, max(ring + LAGS[-1], wide + WIDE_LAGS[-1]), dispatch, 0)
+    lax.fori_loop(0, max(ring + LAGS[-1], wide * STRIDE + WIDE_LAGS[-1]), dispatch, 0)
 
     gate_val = acc_gate[...]
     hidden[...] = (gate_val / (F32(1.0) + jnp.exp(-gate_val)) * acc_up[...]).astype(BF16)
@@ -283,7 +299,17 @@
         part[...] = value.reshape(part.shape)
         wait(pair.at[k], pair_sem.at[k])
         send_far[k] = (part[far] + pair[k, far].astype(F32)).astype(BF16)
-        send(send_far.at[k], got_far.at[k], 6, far_sem.at[k], at(y, z, xb, c))
+
+        @pl.when(k < relayed)
+        def _():
+            send(send_far.at[k], got_far.at[k], 6, far_sem.at[k], at(y, z, xb, c))
+
+        @pl.when(k >= relayed)
+        def _():
+            send(send_far.at[k], got_far.at[k], 6, far_sem.at[k], at(y, z, far, c))
+            send_b[k] = (part[xb] + pair[k, xb].astype(F32)).astype(BF16)
+            send(send_b.at[k], got_f.at[k], 10, rf_sem.at[k], at(y, z, xb, c))
+
         send_f[k] = (part[xf] + pair[k, xf].astype(F32)).astype(BF16)
         send(send_f.at[k], got_b.at[k], 9, rb_sem.at[k], at(y, z, xf, c))
         keep_b[k] = part[xb] + pair[k, xb].astype(F32)
@@ -295,6 +321,11 @@
         send(send_b.at[k], got_f.at[k], 10, rf_sem.at[k], at(y, z, xb, c))
 
     def reduce_end(k):
+        @pl.when(k >= relayed)
+        def _():
+            wait(got_far.at[k], far_sem.at[k])
+            keep_own[k] = keep_own[k] + got_far[k].astype(F32)
+
         wait(got_b.at[k], rb_sem.at[k])
         wait(got_f.at[k], rf_sem.at[k])
         value = keep_own[k] + got_b[k].astype(F32) + got_f[k].astype(F32)
@@ -361,19 +392,19 @@
 
     def combine(t, carry):
         run(t, BACK_LAGS[0], ring, partial_sum)
-        run(t, WIDE_BACK_LAGS[0], wide, lambda j: partial_sum(ring + j))
+        run_wide(t, WIDE_BACK_LAGS[0], lambda j: partial_sum(ring + j))
         run(t, BACK_LAGS[1], ring, reduce_start)
-        run(t, WIDE_BACK_LAGS[1], wide, wide_back)
-        run(t, BACK_LAGS[2], ring, reduce_forward)
-        run(t, WIDE_BACK_LAGS[2], wide, wide_blend)
+        run_wide(t, WIDE_BACK_LAGS[1], wide_back)
+        run(t, BACK_LAGS[2], relayed, reduce_forward)
+        run_wide(t, WIDE_BACK_LAGS[2], wide_blend)
         run(t, BACK_LAGS[3], ring, reduce_end)
-        run(t, WIDE_BACK_LAGS[3], wide, wide_sum)
+        run_wide(t, WIDE_BACK_LAGS[3], wide_sum)
         run(t, BACK_LAGS[4], ring, blend_rows)
-        run(t, WIDE_BACK_LAGS[4], wide, wide_finish)
+        run_wide(t, WIDE_BACK_LAGS[4], wide_finish)
         run(t, BACK_LAGS[5], ring, finish)
         return carry
 
-    lax.fori_loop(0, max(ring + BACK_LAGS[-1], wide + WIDE_BACK_LAGS[-1]), combine, 0)
+    lax.fori_loop(0, max(ring + BACK_LAGS[-1], wide * STRIDE + WIDE_BACK_LAGS[-1]), combine, 0)
 
     wait(meta.at[x, pl.ds(0, zs - 1)], send_sem.at[0])
     wait(zbuf.at[:, pl.ds(0, zs - 1)], send_sem.at[1])

time: 90 us -> 88.6 us (0.984)
  no operation moved by 1% of the time
where the time goes in v3:
time: 88.6 us; the launch traced here: 88.5 us
  Pallas kernels  87 us (98%)
  local copies, waits for them, and re-layouts  1.46 us (2%)
    pallas_call x1, Pallas kernels, on_device(): pl.pallas_call(functools.partial(kernel, groups, zs, xs, rows, chunks), o...  87 us

profile of v3, /device:TPU:6, one launch (start us, length us, event | category | flops | bytes accessed | tf_op | source)
XLA Modules:
  0.0 88.5 jit_solution(16998792693539056179)
XLA Ops:
  0.0 87.0 %shard_map.64 = bf16[4,7168]{1,0:T(4,128)(2,1)} custom-call(bf16[4,7168]{1,0:T(4,128)(2,1)} %tok_ref.1, s32[4,8]{1,0:T(4,128)} %ids_ref.1, bf16[4,8]{1,0:T(4,128)(2,1)} %gates_ref.1, bf16[1,7168,256]{2,1,0:T(8,128)(2,1)} %gate_hbm.1, bf16[1,7168,256]{2,1,0:T(8,128)(2,1)} %up_hbm.1, bf16[1,256,7168]{2,1,0:T(8,128)(2,1)} %down_hbm.1), custom_call_target="tpu_custom_call" | custom-call | tf_op jit(solution)/shard_map/pallas_call | solution.py:446
  87.0 1.5 %copy.8 = bf16[4,7168]{1,0:T(4,128)(2,1)} copy(bf16[4,7168]{1,0:T(4,128)(2,1)} %shard_map.64) | data formatting | bytes 114688
